TPU v7x, 512 devices: a whole 4x8x8 slice. The times are simulated.
512 devices in a mesh: var: 32 (over x, y), tp: 16 (over z, core).
Axes of the slice: x: 4, y: 8, z: 8, core: 2. Of those that a mesh axis runs over, the one named last changes fastest.
Arguments:
- projected: bfloat16 [1024, 32, 3, 8192], P(('var', 'tp')), may hold values from -6 to 6
- cache_history: bfloat16 [192, 127, 8192], P('var', None, 'tp'), may hold values from -6 to 6
- cache_inputs: bfloat16 [192, 6, 3, 8192], P('var', None, None, 'tp'), may hold values from -6 to 6
- feature_taps: bfloat16 [7, 3, 8192], P(None, None, 'tp'), may hold values from -2 to 2
- filters: bfloat16 [128, 512], P(None, 'tp'), may hold values from -0.5 to 0.5
- skip_weight: bfloat16 [8192], P('tp'), may hold values from -4 to 4
- base_inputs: bfloat16 [4, 3, 8192], P(None, None, 'tp'), may hold values from -6 to 6
- window_owner: int32 [1024, 1], replicated, may hold values from 0 to 31; in each aligned block of 32 rows (0 to 31, 32 to 63, ...) at most 2 rows name the same one
- window_slot: int32 [1024], replicated, may hold values from 0 to 5
- variant_position: int32 [1024], P('var'), may hold values from 0 to 31
- allele: int32 [1024], P('var'), may hold values from 0 to 3
Outputs:
- mixer_out: bfloat16 [1024, 32, 8192], P(('var', 'tp'))
Inputs may be any that keep to these rules, and one draw needn't show every extreme that they name: `window_owner`: among the windows of one index of var (aligned blocks of 32 rows), at most 2 name the same owner.
All inputs are finite; a program needn't handle non-finite values.
Results may differ from a plain program's by a relative error of at most 0.0049.
Values may be sent and summed in bfloat16 or wider, within the bound.
No kernel may reach another device: no remote copies, remote signals or barrier semaphores. Data moves between devices by JAX's collectives and lax.ppermute only.
A program may use at most 128 MiB of HBM per device.

v0:
```python
import jax
import jax.numpy as jnp
from jax import lax
from jax.sharding import PartitionSpec as P


def tap_table(filters, row_count, col_count, offset):
    tap_count = filters.shape[0]
    lag_index = jnp.arange(row_count)[:, None] + offset - jnp.arange(col_count)[None, :]
    onehot = (lag_index[:, :, None] == jnp.arange(tap_count)[None, None, :]).astype(jnp.bfloat16)
    return jnp.einsum("tsj,jg->gts", onehot, filters, preferred_element_type=jnp.float32).astype(
        jnp.bfloat16
    )


def apply_table(table, values, group_size):
    item_count, length, channel_width = values.shape
    grouped = values.reshape(item_count, length, channel_width // group_size, group_size)
    result = jnp.einsum("gts,nsgc->ntgc", table, grouped, preferred_element_type=jnp.float32)
    return result.reshape(item_count, table.shape[1], channel_width)


def featurize(extended, feature_taps, window_len):
    item_count, ext_len, stream_count, channel_width = extended.shape
    wide = stream_count * channel_width
    flat_in = extended.reshape(item_count, ext_len, wide)
    kernel = feature_taps[::-1].reshape(feature_taps.shape[0], 1, wide)
    result = lax.conv_general_dilated(
        flat_in,
        kernel,
        window_strides=(1,),
        padding="VALID",
        dimension_numbers=("NWC", "WIO", "NWC"),
        feature_group_count=wide,
        preferred_element_type=jnp.float32,
    )
    return result.reshape(item_count, window_len, stream_count, channel_width)


def local(
    projected,
    cache_history,
    cache_inputs,
    feature_taps,
    filters,
    skip_weight,
    base_inputs,
    window_owner,
    window_slot,
    variant_position,
    allele,
):
    var_count = lax.axis_size("var")
    my_index = lax.axis_index("var")
    local_windows = variant_position.shape[0]
    capacity = max(2, 2 * local_windows // var_count)
    window_len = projected.shape[1]
    history_len = cache_history.shape[1]
    channel_width = cache_history.shape[2]
    group_size = channel_width // filters.shape[1]
    owners_all = window_owner[:, 0].reshape(var_count, local_windows)
    slots_all = window_slot.reshape(var_count, local_windows)
    same_owner = (
        owners_all[:, :, None] == jnp.arange(var_count, dtype=jnp.int32)[None, None, :]
    ).astype(jnp.int32)
    earlier = jnp.cumsum(same_owner, axis=1) - same_owner
    rank_all = jnp.sum(earlier * same_owner, axis=2)
    matches = (owners_all[:, None, :] == my_index) & (
        rank_all[:, None, :] == jnp.arange(capacity, dtype=jnp.int32)[None, :, None]
    )
    slot_pick = jnp.sum(jnp.where(matches, slots_all[:, None, :], 0), axis=2).reshape(-1)
    own_owner = lax.dynamic_index_in_dim(owners_all, my_index, 0, keepdims=False)
    own_rank = lax.dynamic_index_in_dim(rank_all, my_index, 0, keepdims=False)
    source_row = own_owner * capacity + own_rank
    lead_send = jnp.take(cache_inputs, slot_pick, axis=0).reshape(
        (var_count, capacity) + cache_inputs.shape[1:]
    )
    history_send = jnp.take(cache_history, slot_pick, axis=0).reshape(
        var_count, capacity, history_len, channel_width
    )
    history_got, lead_got = (
        lax.all_to_all(history_send, "var", split_axis=0, concat_axis=0, tiled=True),
        lax.all_to_all(lead_send, "var", split_axis=0, concat_axis=0, tiled=True),
    )
    history_mine = jnp.take(
        history_got.reshape(var_count * capacity, history_len, channel_width), source_row, axis=0
    )
    table_pre = tap_table(filters, window_len, history_len, history_len)
    carried = lax.optimization_barrier(
        apply_table(table_pre, history_mine, group_size).astype(jnp.bfloat16)
    )
    lead_mine = jnp.take(
        lead_got.reshape((var_count * capacity,) + lead_got.shape[2:]), source_row, axis=0
    )
    channels = lax.all_to_all(projected, "tp", split_axis=3, concat_axis=0, tiled=True)
    allele_hot = (allele[:, None] == jnp.arange(base_inputs.shape[0])[None, :]).astype(jnp.bfloat16)
    base_rows = jnp.einsum(
        "wb,bsc->wsc", allele_hot, base_inputs, preferred_element_type=jnp.float32
    ).astype(jnp.bfloat16)
    placed = jnp.arange(window_len)[None, :] == variant_position[:, None]
    altered = jnp.where(placed[:, :, None, None], base_rows[:, None], channels)
    extended = jnp.concatenate([lead_mine, altered], axis=1)
    featured = featurize(extended, feature_taps, window_len)
    mixed_in = lax.optimization_barrier(
        (featured[:, :, 1] * featured[:, :, 2]).astype(jnp.bfloat16)
    )
    table_win = tap_table(filters, window_len, window_len, 0)
    inside = apply_table(table_win, mixed_in, group_size)
    filtered = (
        inside
        + carried.astype(jnp.float32)
        + skip_weight.astype(jnp.float32) * mixed_in.astype(jnp.float32)
    )
    mixer_out = (featured[:, :, 0] * filtered).astype(jnp.bfloat16)
    return lax.all_to_all(mixer_out, "tp", split_axis=0, concat_axis=2, tiled=True)


def solution(mesh):
    return jax.shard_map(
        local,
        mesh=mesh,
        in_specs=(
            P(("var", "tp"), None, None, None),
            P("var", None, "tp"),
            P("var", None, None, "tp"),
            P(None, None, "tp"),
            P(None, "tp"),
            P("tp"),
            P(None, None, "tp"),
            P(),
            P(),
            P("var"),
            P("var"),
        ),
        out_specs=P(("var", "tp"), None, None),
        check_vma=False,
    )
```

profile of v0, /device:TPU:29, one launch (start us, length us, event | category | flops | bytes accessed | tf_op | source)
XLA Modules:
  0.0 421.7 jit_solution(15983807273847212146)
XLA Ops:
  0.0 0.5 broadcast.144
  0.5 1.3 reduce.6
  2.0 1.0 fusion.32
  3.1 0.8 broadcast_in_dim.91
  4.4 2.8 gather_fusion
  7.2 1.5 broadcast_select_fusion.2
  8.6 1.8 copy.99
  10.5 9.3 %all-to-all-start = ((bf16[32,2,6,3,512]{4,1,3,2,0:T(2,128)(2,1)}), bf16[32,2,6,3,512]{4,1,3,2,0:T(2,128)(2,1)S(1)}, u32[]{:S(2)}, u32[]{:S(2)}) async-start(bf16[32,2,6,3,512]{4,1,3,2,0:T(2,128)(2,1)} %copy.99), calls=%async_computation | async-start | bytes 2359296 | tf_op jit(solution)/shard_map/all_to_all | solution.py:83
  19.8 20.1 %copy.103 = bf16[2,32,3,8192]{1,2,0,3:T(4,128)(2,1)} copy(bf16[2,32,3,8192]{3,1,2,0:T(8,128)(2,1)} %param.11) | data formatting | bytes 6291456 | tf_op args[0]
  39.9 18.3 %reshape.242 = bf16[16,2,49152]{2,1,0:T(2,128)(2,1)} reshape(bf16[8192,2,3,32]{3,2,1,0:T(4,128)(2,1)} %bitcast.62) | data formatting | bytes 6291456
  58.1 11.6 %all-to-all-start.1 = ((bf16[16,2,49152]{2,1,0:T(2,128)(2,1)}), bf16[16,2,49152]{2,1,0:T(2,128)(2,1)}, u32[]{:S(2)}, u32[]{:S(2)}) async-start(bf16[16,2,49152]{2,1,0:T(2,128)(2,1)} %reshape.242), calls=%async_computation.1 | async-start | bytes 6291456 | tf_op jit(solution)/shard_map/all_to_all | solution.py:95
  69.7 5.3 %gather_fusion.2 = bf16[64,127,512]{2,1,0:T(8,128)(2,1)} fusion(bf16[6,127,512]{2,1,0:T(8,128)(2,1)S(1)} %copy-done, s32[1024]{0:T(1024)S(1)} %pad_clamp_fusion.1), kind=kCustom, calls=%fused_computation.2 | custom fusion | bytes 16646400 | tf_op jit(solution)/shard_map/jit(_take)/gather | solution.py:78
  75.0 7.5 %broadcast_select_fusion = bf16[32,2,127,512]{3,2,1,0:T(8,128)(2,1)} fusion(bf16[32,2,127,512]{3,2,1,0:T(8,128)(2,1)} %bitcast.63, pred[32,2]{1,0:T(8,128)(4,1)S(1)} %copy.96), kind=kLoop, calls=%fused_computation.4 | loop fusion | flops 4161536 | bytes 16646208 | tf_op jit(solution)/shard_map/jit(_take)/select_n | solution.py:78
  82.5 16.3 %copy.112 = bf16[32,2,127,512]{3,1,2,0:T(2,128)(2,1)} copy(bf16[32,2,127,512]{3,2,1,0:T(8,128)(2,1)} %broadcast_select_fusion) | data formatting | bytes 16646144 | tf_op jit(solution)/shard_map/jit(_take)/select_n | solution.py:78
  98.8 41.9 %all-to-all-done.1 = bf16[16,2,49152]{2,1,0:T(2,128)(2,1)} async-done(((bf16[16,2,49152]{2,1,0:T(2,128)(2,1)}), bf16[16,2,49152]{2,1,0:T(2,128)(2,1)}, u32[]{:S(2)}, u32[]{:S(2)}) %all-to-all-start.1) | async-done | bytes 3145760 | tf_op jit(solution)/shard_map/all_to_all | solution.py:95
  140.8 9.3 %all-to-all-start.2 = ((bf16[32,2,127,512]{3,1,2,0:T(2,128)(2,1)}), bf16[32,2,127,512]{3,1,2,0:T(2,128)(2,1)}, u32[]{:S(2)}, u32[]{:S(2)}) async-start(bf16[32,2,127,512]{3,1,2,0:T(2,128)(2,1)} %copy.112), calls=%async_computation.2 | async-start | bytes 16646144 | tf_op jit(solution)/shard_map/all_to_all | solution.py:82
  150.1 0.2 fusion.15
  150.3 0.7 copy.130
  151.0 1.3 rev.3
  152.2 0.3 fusion.13
  152.6 1.1 copy.120
  154.0 1.6 fusion.14
  155.6 0.3 copy.100
  156.0 0.6 gather_fusion.1
  156.6 0.4 copy.101
  157.0 0.8 gather.27
  157.9 16.8 %reshape.243 = bf16[8192,2,3,32]{3,2,1,0:T(4,128)(2,1)} reshape(bf16[16,2,49152]{2,1,0:T(2,128)(2,1)} %all-to-all-done.1) | data formatting | bytes 6291456
  174.7 25.1 %copy.104 = bf16[2,32,3,16,512]{4,2,1,0,3:T(4,128)(2,1)} copy(bf16[2,32,3,16,512]{1,2,0,4,3:T(4,128)(2,1)} %bitcast.61) | data formatting | bytes 6291456 | tf_op jit(solution)/shard_map/all_to_all | solution.py:95
  199.9 9.7 %all_to_all.36 = bf16[32,32,1536]{2,1,0:T(8,128)(2,1)} reshape(bf16[16,2,32,3,512]{4,3,2,1,0:T(4,128)(2,1)} %bitcast.66) | data formatting | bytes 6291456 | tf_op jit(solution)/shard_map/all_to_all | solution.py:95
  209.6 5.5 %copy_select_fusion = bf16[32,32,1536]{2,0,1:T(8,128)(2,1)S(1)} fusion(bf16[32,32,1536]{2,1,0:T(8,128)(2,1)} %all_to_all.36, pred[32,32]{0,1:T(8,128)(4,1)S(1)} %iota_compare_fusion.11, bf16[32,1536]{1,0:T(8,128)(2,1)S(1)} %bitcast.75), kind=kLoop, calls=%fused_computation.12 | loop fusion | flops 1572864 | bytes 6390784 | tf_op jit(solution)/shard_map/jit(_where)/select_n | solution.py:101
  215.0 3.7 fusion.2
  218.8 6.3 %copy.107 = f32[32,32,1536]{2,1,0:T(8,128)} copy(f32[32,32,1536]{2,0,1:T(8,128)S(1)} %fusion.2) | data formatting | bytes 12582912 | tf_op jit(solution)/shard_map/conv_general_dilated | solution.py:28
  225.1 11.3 %reshape.191 = f32[32,32,3,512]{3,2,1,0:T(4,128)} reshape(f32[32,32,1536]{2,1,0:T(8,128)} %copy.107) | data formatting | bytes 12582912 | tf_op jit(solution)/shard_map/reshape | solution.py:37
  236.4 14.3 %fusion.9 = (bf16[32,32,1,512]{3,2,1,0:T(2,128)(2,1)S(1)}, f32[32,32,1,512]{3,2,1,0:T(1,128)}) fusion(f32[32,32,3,512]{3,2,1,0:T(4,128)} %reshape.191), kind=kLoop, calls=%fused_computation.16 | loop fusion | flops 1048576 | bytes 9437184 | tf_op jit(solution)/shard_map/convert_element_type | solution.py:105
  250.7 0.3 copy.144
  251.0 6.4 %copy.123 = bf16[32,32,512]{1,0,2:T(8,128)(2,1)} copy(bf16[32,32,512]{2,1,0:T(8,128)(2,1)S(1)} %bitcast.70) | data formatting | bytes 2097152 | tf_op jit(solution)/shard_map/reshape | solution.py:18
  257.5 6.6 %fusion.33 = f32[32,32,16,32]{3,1,2,0:T(8,128)} fusion(bf16[32,32,32,16]{1,0,3,2:T(8,128)(2,1)} %bitcast.67, bf16[32,32,32,1]{2,1,3,0:T(8,128)(2,1)S(1)} %copy-done.2), kind=kOutput, calls=%fused_computation.65 | convolution fusion | flops 33554432 | bytes 3211264 | tf_op jit(solution)/shard_map/gts,nsgc->ntgc/dot_general | solution.py:19
  264.1 6.3 %copy.118 = f32[32,32,512]{2,1,0:T(8,128)} copy(f32[32,32,512]{1,0,2:T(8,128)} %bitcast.64) | data formatting | bytes 4194304 | tf_op jit(solution)/shard_map/reshape | solution.py:20
  270.4 65.7 %all-to-all-done.2 = bf16[32,2,127,512]{3,1,2,0:T(2,128)(2,1)} async-done(((bf16[32,2,127,512]{3,1,2,0:T(2,128)(2,1)}), bf16[32,2,127,512]{3,1,2,0:T(2,128)(2,1)}, u32[]{:S(2)}, u32[]{:S(2)}) %all-to-all-start.2) | async-done | bytes 8323104 | tf_op jit(solution)/shard_map/all_to_all | solution.py:82
  336.1 8.6 %copy.113 = bf16[32,2,127,512]{3,2,1,0:T(8,128)(2,1)} copy(bf16[32,2,127,512]{3,1,2,0:T(2,128)(2,1)} %all-to-all-done.2) | data formatting | bytes 16646144 | tf_op jit(solution)/shard_map/all_to_all | solution.py:82
  344.7 6.1 %gather_fusion.3 = bf16[32,127,512]{2,1,0:T(8,128)(2,1)} fusion(bf16[64,127,512]{2,1,0:T(8,128)(2,1)} %bitcast.65, s32[1024]{0:T(1024)S(1)} %pad_clamp_fusion), kind=kCustom, calls=%fused_computation.3 | custom fusion | bytes 8323200 | tf_op jit(solution)/shard_map/jit(_take)/gather | solution.py:85
  350.9 6.5 %copy.114 = bf16[32,127,512]{1,2,0:T(8,128)(2,1)} copy(bf16[32,127,512]{2,1,0:T(8,128)(2,1)} %gather_fusion.3) | data formatting | bytes 8323072 | tf_op jit(solution)/shard_map/jit(_take)/gather | solution.py:85
  357.4 2.7 broadcast_select_fusion.1
  360.1 4.8 %fusion.6 = bf16[32,32,16,32]{3,1,2,0:T(8,128)(2,1)} fusion(bf16[32,127,32,16]{1,3,2,0:T(8,128)(2,1)S(1)} %broadcast_select_fusion.1, bf16[32,32,127,1]{2,0,1,3:T(8,128)(2,1)S(1)} %copy-done.4), kind=kOutput, calls=%fused_computation.13 | convolution fusion | flops 133693440 | bytes 5470208 | tf_op jit(solution)/shard_map/gts,nsgc->ntgc/dot_general | solution.py:19
  364.9 4.4 %copy.117 = bf16[32,32,512]{2,1,0:T(8,128)(2,1)S(1)} copy(bf16[32,32,512]{1,0,2:T(8,128)(2,1)} %bitcast.68) | data formatting | bytes 2097152 | tf_op jit(solution)/shard_map/optimization_barrier | solution.py:89
  369.3 3.1 fusion.10
  372.4 48.3 %all_to_all.46 = bf16[32,32,512]{2,1,0:T(8,128)(2,1)S(1)} all-to-all(bf16[32,32,512]{2,1,0:T(8,128)(2,1)S(1)} %fusion.10), channel_id=1, replica_groups=mesh['var'=32,'tp'=16] {'tp'}, dimensions={0} | all-to-all | bytes 2097152 | tf_op jit(solution)/shard_map/all_to_all | solution.py:115
  420.7 1.1 copy.131
  (46 shorter events, 1.1 us)
Async XLA Ops:
  0.0 69.7 %copy-start = (bf16[6,127,512]{2,1,0:T(8,128)(2,1)S(1)}, bf16[6,127,512]{2,1,0:T(8,128)(2,1)}, u32[]{:S(2)}) copy-start(bf16[6,127,512]{2,1,0:T(8,128)(2,1)} %param.12) | copy-start | bytes 2340868
  10.5 47.7 %all-to-all-start = ((bf16[32,2,6,3,512]{4,1,3,2,0:T(2,128)(2,1)}), bf16[32,2,6,3,512]{4,1,3,2,0:T(2,128)(2,1)S(1)}, u32[]{:S(2)}, u32[]{:S(2)}) async-start(bf16[32,2,6,3,512]{4,1,3,2,0:T(2,128)(2,1)} %copy.99), calls=%async_computation | async-start | bytes 2359296 | tf_op jit(solution)/shard_map/all_to_all | solution.py:83
  58.1 82.6 %all-to-all-start.1 = ((bf16[16,2,49152]{2,1,0:T(2,128)(2,1)}), bf16[16,2,49152]{2,1,0:T(2,128)(2,1)}, u32[]{:S(2)}, u32[]{:S(2)}) async-start(bf16[16,2,49152]{2,1,0:T(2,128)(2,1)} %reshape.242), calls=%async_computation.1 | async-start | bytes 6291456 | tf_op jit(solution)/shard_map/all_to_all | solution.py:95
  98.8 51.3 %copy-start.7 = (bf16[4,3,512]{2,0,1:T(4,128)(2,1)S(1)}, bf16[4,3,512]{2,0,1:T(4,128)(2,1)}, u32[]{:S(2)}) copy-start(bf16[4,3,512]{2,0,1:T(4,128)(2,1)} %param.17) | copy-start | bytes 36868
  98.8 51.3 %copy-start.10 = (s32[32]{0:T(128)S(1)}, s32[32]{0:T(128)}, u32[]{:S(2)}) copy-start(s32[32]{0:T(128)} %param.21) | copy-start | bytes 388
  98.8 52.2 %copy-start.5 = (bf16[7,3,512]{2,0,1:T(8,128)(2,1)S(1)}, bf16[7,3,512]{2,0,1:T(8,128)(2,1)}, u32[]{:S(2)}) copy-start(bf16[7,3,512]{2,0,1:T(8,128)(2,1)} %param.14) | copy-start | bytes 64516
  98.8 53.4 %copy-start.8 = (bf16[128,32]{0,1:T(8,128)(2,1)S(1)}, bf16[128,32]{0,1:T(8,128)(2,1)}, u32[]{:S(2)}) copy-start(bf16[128,32]{0,1:T(8,128)(2,1)} %param.15) | copy-start | bytes 24580
  98.8 54.9 %copy-start.9 = (bf16[512]{0:T(512)(128)(2,1)S(1)}, bf16[512]{0:T(512)(128)(2,1)}, u32[]{:S(2)}) copy-start(bf16[512]{0:T(512)(128)(2,1)} %param.16) | copy-start | bytes 3076
  98.8 56.8 %copy-start.11 = (s32[32]{0:T(128)S(1)}, s32[32]{0:T(128)}, u32[]{:S(2)}) copy-start(s32[32]{0:T(128)} %param.20) | copy-start | bytes 388
  140.8 195.4 %all-to-all-start.2 = ((bf16[32,2,127,512]{3,1,2,0:T(2,128)(2,1)}), bf16[32,2,127,512]{3,1,2,0:T(2,128)(2,1)}, u32[]{:S(2)}, u32[]{:S(2)}) async-start(bf16[32,2,127,512]{3,1,2,0:T(2,128)(2,1)} %copy.112), calls=%async_computation.2 | async-start | bytes 16646144 | tf_op jit(solution)/shard_map/all_to_all | solution.py:82
  199.9 9.7 %copy-start.3 = (bf16[3,4,8,512]{3,2,0,1:T(8,128)(2,1)S(1)}, bf16[3,4,8,512]{3,2,0,1:T(8,128)(2,1)}, u32[]{:S(2)}) copy-start(bf16[3,4,8,512]{3,2,0,1:T(8,128)(2,1)} %copy.130) | copy-start | bytes 294916
  209.6 5.5 %copy-start.6 = (bf16[7,3,512]{2,0,1:T(8,128)(2,1)S(1)}, bf16[7,3,512]{2,0,1:T(8,128)(2,1)}, u32[]{:S(2)}) copy-start(bf16[7,3,512]{2,0,1:T(8,128)(2,1)} %rev.3) | copy-start | bytes 64516
  250.7 6.8 %copy-start.2 = (bf16[32,32,32,1]{2,1,3,0:T(8,128)(2,1)S(1)}, bf16[32,32,32,1]{2,1,3,0:T(8,128)(2,1)}, u32[]{:S(2)}) copy-start(bf16[32,32,32,1]{2,1,3,0:T(8,128)(2,1)} %copy.120) | copy-start | bytes 196612
  357.4 2.7 copy-start.4
  369.3 52.4 %copy-start.1 = (bf16[6,127,512]{2,1,0:T(8,128)(2,1)S(1)}, bf16[6,127,512]{2,1,0:T(8,128)(2,1)}, u32[]{:S(2)}) copy-start(bf16[6,127,512]{2,1,0:T(8,128)(2,1)} %param.12) | copy-start | bytes 2340868
where the time goes:
time: 425 us; the launch traced here: 422 us
  local copies, waits for them, and re-layouts  181 us (43%)
  waiting for transfers between devices  108 us (25%)
  blocking collectives  48.3 us (11%)
  other arithmetic  37.4 us (9%)
  starting transfers between devices  30.2 us (7%)
  matrix products  17.3 us (4%)
    all_to_all x1, waiting for transfers between devices, local(): lax.all_to_all(history_send, 'var', split_axis=0, concat_axis=0, tiled=True)  65.7 us
    unnamed x29, local copies, waits for them, and re-layouts  56 us
    all_to_all x1, blocking collectives, local(): lax.all_to_all(mixer_out, 'tp', split_axis=0, concat_axis=2, tiled=True)  48.3 us
    all_to_all x1, waiting for transfers between devices, local(): lax.all_to_all(projected, 'tp', split_axis=3, concat_axis=0, tiled=True)  41.9 us
    all_to_all x2, local copies, waits for them, and re-layouts, local(): lax.all_to_all(projected, 'tp', split_axis=3, concat_axis=0, tiled=True)  34.8 us
    select_n x1, local copies, waits for them, and re-layouts, local(): jnp.take(cache_history, slot_pick, axis=0)  16.3 us
    convert_element_type x1, other arithmetic, local(): (featured[:, :, 1] * featured[:, :, 2]).astype(jnp.bfloat16)  14.3 us
    gather x2, local copies, waits for them, and re-layouts, local(): jnp.take(history_got.reshape(var_count * capacity, history_len, channel_w...  12.7 us
  transfers between devices with their start and end apart: 3, of which 2 were waited for; matrix products, arithmetic and copies ran while one was open for 42% of the time, Pallas kernels for 0%

commit v1 on v0

v1 whole, which is shorter than its diff:
```python
import functools
import jax
import jax.numpy as jnp
from jax import lax
from jax.experimental import pallas as pl
from jax.experimental.pallas import tpu as pltpu
from jax.sharding import PartitionSpec as P

LANES = 128
TAP_ROWS = 40
TIME = 32


def owner_kernel(group_size, history_ref, inputs_ref, filters_ref, taps_ref, base_ref, skip_ref,
                 lead_ref, carried_ref, param_ref, line_scr, lead_scr, param_scr):
    loci, history_len, width = history_ref.shape
    lead_len, streams = inputs_ref.shape[1:3]
    taps, bases = taps_ref.shape[1], base_ref.shape[1]
    groups, tap_count = filters_ref.shape
    blocks = width // LANES
    per_block = LANES // group_size
    f32 = jnp.float32
    for n in range(loci):
        for r in range(lead_len):
            for b in range(blocks):
                at = ((n * blocks + b) * lead_len + r) * streams
                piece = inputs_ref[n, r, :, b * LANES : (b + 1) * LANES]
                lead_scr[at : at + streams, :] = piece.astype(f32)
    span = blocks * lead_len * streams
    for n in range(loci):
        lead_ref[n] = lead_scr[n * span : (n + 1) * span, :].astype(jnp.bfloat16)
    param_scr[...] = jnp.zeros_like(param_scr)
    for s in range(streams):
        param_scr[s * taps : (s + 1) * taps, :] = taps_ref[s].astype(f32)
        at = streams * taps + s * bases
        param_scr[at : at + bases, :] = base_ref[s].astype(f32)
    at = streams * (taps + bases)
    param_scr[at : at + 1, :] = skip_ref[...].astype(f32)
    owner = lax.broadcasted_iota(jnp.int32, (groups, width), 1) // group_size
    spread = (owner == lax.broadcasted_iota(jnp.int32, (groups, width), 0)).astype(jnp.bfloat16)
    wide = lax.dot_general(
        filters_ref[...], spread, (((0,), (0,)), ((), ())), preferred_element_type=f32
    )
    param_ref[:TAP_ROWS, :] = param_scr[...].astype(jnp.bfloat16)
    param_ref[TAP_ROWS:, :] = wide[:TIME].astype(jnp.bfloat16)

    row = lax.broadcasted_iota(jnp.int32, (tap_count, tap_count), 0)
    col = lax.broadcasted_iota(jnp.int32, (tap_count, tap_count), 1)
    flip = (row + col == tap_count - 1).astype(jnp.bfloat16)
    line_scr[...] = jnp.dot(filters_ref[...], flip, preferred_element_type=f32)
    t_row = lax.broadcasted_iota(jnp.int32, (TIME, tap_count), 0)
    s_col = lax.broadcasted_iota(jnp.int32, (TIME, tap_count), 1)
    valid = (s_col >= t_row) & (s_col < history_len)
    lane = lax.broadcasted_iota(jnp.int32, (TIME, LANES), 1) // group_size
    for b in range(blocks):
        tables = []
        for g in range(per_block):
            index = b * per_block + g
            line = jnp.broadcast_to(line_scr[index : index + 1, :], (TIME, tap_count))
            turned = pltpu.roll(line, 0, 1, stride=1, stride_axis=0)
            tables.append(jnp.where(valid, turned, 0.0))
        table = jnp.concatenate(tables, axis=0).astype(jnp.bfloat16)[:, :history_len]
        for n in range(loci):
            past = history_ref[n, :, b * LANES : (b + 1) * LANES]
            full = jnp.dot(table, past, preferred_element_type=f32)
            total = jnp.zeros((TIME, LANES), f32)
            for g in range(per_block):
                total = jnp.where(lane == g, full[g * TIME : (g + 1) * TIME], total)
            carried_ref[n, b * TIME : (b + 1) * TIME, :] = total.astype(jnp.bfloat16)


def owner_of(history, inputs, filters_t, taps, base, skip, group_size):
    loci, _, width = history.shape
    lead_len, streams = inputs.shape[1:3]
    blocks = width // LANES
    shape = lambda *dims: jax.ShapeDtypeStruct(dims, jnp.bfloat16)
    return pl.pallas_call(
        functools.partial(owner_kernel, group_size),
        out_shape=(
            shape(loci, blocks * lead_len * streams, LANES),
            shape(loci, blocks * TIME, LANES),
            shape(TAP_ROWS + TIME, width),
        ),
        in_specs=[pl.BlockSpec(memory_space=pltpu.VMEM)] * 6,
        out_specs=[pl.BlockSpec(memory_space=pltpu.VMEM)] * 3,
        scratch_shapes=[
            pltpu.VMEM(filters_t.shape, jnp.float32),
            pltpu.VMEM((loci * blocks * lead_len * streams, LANES), jnp.float32),
            pltpu.VMEM((TAP_ROWS, width), jnp.float32),
        ],
        name="owner",
    )(history, inputs, filters_t, taps, base, skip)


def mixer_kernel(dims, pos_ref, allele_ref, proj_ref, lead_ref, carried_ref, param_ref,
                 out_ref, x_scr, l_scr, c_scr, p_scr, f_scr, m_scr, o_scr):
    taps, bases, streams, lead_len = dims
    wins, _, _, width = proj_ref.shape
    blocks = width // LANES
    rows = wins * blocks
    lead_rows = lead_len * streams
    f32 = jnp.float32
    for w in range(wins):
        for b in range(blocks):
            q = w * blocks + b
            lanes = slice(b * LANES, (b + 1) * LANES)
            p_scr[q * TAP_ROWS : (q + 1) * TAP_ROWS, :] = param_ref[0, :TAP_ROWS, lanes].astype(f32)
            f_scr[q * TIME : (q + 1) * TIME, :] = param_ref[0, TAP_ROWS:, lanes].astype(f32)
            for s in range(streams):
                x_scr[s, q * TIME : (q + 1) * TIME, :] = proj_ref[w, s, :, lanes].astype(f32)
        span = blocks * lead_rows
        l_scr[w * span : (w + 1) * span, :] = lead_ref[0, w].astype(f32)
        span = blocks * TIME
        c_scr[w * span : (w + 1) * span, :] = carried_ref[0, w].astype(f32)
    for w in range(wins):
        for s in range(streams):
            for b in range(blocks):
                q = w * blocks + b
                source = q * TAP_ROWS + streams * taps + s * bases + allele_ref[w]
                x_scr[s, pl.ds(q * TIME + pos_ref[w], 1), :] = p_scr[pl.ds(source, 1), :]

    def param(r):
        return p_scr[pl.ds(r, rows, stride=TAP_ROWS), :]

    def entry(s, r):
        if r < lead_len:
            return l_scr[pl.ds(r * streams + s, rows, stride=lead_rows), :]
        return x_scr[s, pl.ds(r - lead_len, rows, stride=TIME), :]

    def featured(s):
        weight = [param(s * taps + j) for j in range(taps)]
        window = [entry(s, r) for r in range(taps - 1)]
        for t in range(TIME):
            window.append(entry(s, t + taps - 1))
            total = weight[0] * window[taps - 1]
            for j in range(1, taps):
                total = total + weight[j] * window[taps - 1 - j]
            window.pop(0)
            yield total

    for t, (one, two) in enumerate(zip(featured(1), featured(2))):
        m_scr[t] = (one * two).astype(jnp.bfloat16).astype(f32)
    skip = param(streams * (taps + bases))
    gates = featured(0)
    step = 8
    for start in range(0, TIME, step):
        total = [None] * step
        for j in range(start + step):
            tap = f_scr[pl.ds(j, rows, stride=TIME), :]
            for i in range(step):
                at = start + i - j
                if at >= 0:
                    term = tap * m_scr[at]
                    total[i] = term if total[i] is None else total[i] + term
        for i in range(step):
            t = start + i
            carried = c_scr[pl.ds(t, rows, stride=TIME), :]
            filtered = total[i] + carried + skip * m_scr[t]
            o_scr[pl.ds(t, rows, stride=TIME), :] = next(gates) * filtered
    for w in range(wins):
        for b in range(blocks):
            q = w * blocks + b
            lanes = slice(b * LANES, (b + 1) * LANES)
            out_ref[w, :, lanes] = o_scr[q * TIME : (q + 1) * TIME, :].astype(jnp.bfloat16)


def mixer_of(dims, position, allele, proj, lead, carried, params):
    taps, bases, streams, lead_len = dims
    wins, _, _, total = proj.shape
    parts = params.shape[0]
    width = total // parts
    blocks = width // LANES
    rows = wins * blocks
    spec = pltpu.PrefetchScalarGridSpec(
        num_scalar_prefetch=2,
        grid=(parts,),
        in_specs=[
            pl.BlockSpec((wins, streams, TIME, width), lambda k, *_: (0, 0, 0, k)),
            pl.BlockSpec((1, wins, blocks * lead_len * streams, LANES), lambda k, *_: (k, 0, 0, 0)),
            pl.BlockSpec((1, wins, blocks * TIME, LANES), lambda k, *_: (k, 0, 0, 0)),
            pl.BlockSpec((1, TAP_ROWS + TIME, width), lambda k, *_: (k, 0, 0)),
        ],
        out_specs=pl.BlockSpec((wins, TIME, width), lambda k, *_: (0, 0, k)),
        scratch_shapes=[
            pltpu.VMEM((streams, rows * TIME, LANES), jnp.float32),
            pltpu.VMEM((rows * lead_len * streams, LANES), jnp.float32),
            pltpu.VMEM((rows * TIME, LANES), jnp.float32),
            pltpu.VMEM((rows * TAP_ROWS, LANES), jnp.float32),
            pltpu.VMEM((rows * TIME, LANES), jnp.float32),
            pltpu.VMEM((TIME, rows, LANES), jnp.float32),
            pltpu.VMEM((rows * TIME, LANES), jnp.float32),
        ],
    )
    return pl.pallas_call(
        functools.partial(mixer_kernel, dims),
        out_shape=jax.ShapeDtypeStruct((wins, TIME, total), jnp.bfloat16),
        grid_spec=spec,
        name="mixer",
    )(position, allele, proj, lead, carried, params)

def exchange(packed, window_owner, window_slot, me, windows):
    var_count = lax.axis_size("var")
    capacity = 2
    owners = window_owner[:, 0].reshape(var_count, windows)
    slots = window_slot.reshape(var_count, windows)
    mine = owners == me
    rank = jnp.cumsum(mine.astype(jnp.int32), axis=1) - 1
    hit = mine[:, None, :] & (rank[:, None, :] == jnp.arange(capacity)[None, :, None])
    pick = jnp.sum(jnp.where(hit, slots[:, None, :], 0), axis=2).reshape(-1)
    send = packed.at[pick].get(mode="promise_in_bounds")
    send = send.reshape(var_count, capacity * packed.shape[1], LANES)
    got = lax.all_to_all(send, "var", split_axis=0, concat_axis=0, tiled=True)
    got = got.reshape(var_count * capacity, packed.shape[1], LANES)
    own_owner = lax.dynamic_index_in_dim(owners, me, 0, keepdims=False)
    same = own_owner[:, None] == own_owner[None, :]
    earlier = jnp.arange(windows)[None, :] < jnp.arange(windows)[:, None]
    own_rank = jnp.sum((same & earlier).astype(jnp.int32), axis=1)
    return got.at[own_owner * capacity + own_rank].get(mode="promise_in_bounds")


def local(
    projected,
    cache_history,
    cache_inputs,
    feature_taps,
    filters,
    skip_weight,
    base_inputs,
    window_owner,
    window_slot,
    variant_position,
    allele,
):
    var_count, tp_count = lax.axis_size("var"), lax.axis_size("tp")
    me, part = lax.axis_index("var"), lax.axis_index("tp")
    windows, own = variant_position.shape[0], projected.shape[0]
    width = cache_history.shape[2]
    slots = cache_history.shape[0]
    group_size = width // filters.shape[1]
    lead, carried, params = owner_of(
        cache_history,
        cache_inputs,
        filters.T,
        feature_taps.transpose(1, 0, 2),
        base_inputs.transpose(1, 0, 2),
        skip_weight[None],
        group_size,
    )
    packed = jnp.concatenate([lead, carried], axis=1)
    received = exchange(packed, window_owner, window_slot, me, windows)
    received = received.reshape(tp_count, own * received.shape[1], LANES)
    swapped = lax.all_to_all(received, "tp", split_axis=0, concat_axis=0, tiled=True)
    swapped = swapped.reshape(tp_count, own, -1, LANES)
    params = lax.all_gather(params, "tp", axis=0)
    cut = lead.shape[1]
    position = lax.dynamic_slice(variant_position, (part * own,), (own,))
    letter = lax.dynamic_slice(allele, (part * own,), (own,))
    taps, streams = feature_taps.shape[:2]
    return mixer_of(
        (taps, base_inputs.shape[0], streams, cache_inputs.shape[1]),
        position,
        letter,
        projected.transpose(0, 2, 1, 3),
        swapped[:, :, :cut],
        swapped[:, :, cut:],
        params,
    )


def solution(mesh):
    return jax.shard_map(
        local,
        mesh=mesh,
        in_specs=(
            P(("var", "tp"), None, None, None),
            P("var", None, "tp"),
            P("var", None, None, "tp"),
            P(None, None, "tp"),
            P(None, "tp"),
            P("tp"),
            P(None, None, "tp"),
            P(),
            P(),
            P("var"),
            P("var"),
        ),
        out_specs=P(("var", "tp"), None, None),
        check_vma=False,
    )
```

time: 425 us -> 192 us (0.45)
  the two profiles are of different devices: /device:TPU:29 before, /device:TPU:1 now
where the time goes in v1:
time: 192 us; the launch traced here: 191 us
  waiting for transfers between devices  120 us (62%)
  starting transfers between devices  24.9 us (13%)
  Pallas kernels  19.3 us (10%)
  between operations  13.5 us (7%)
  local copies, waits for them, and re-layouts  10.6 us (6%)
  other arithmetic  2.89 us (2%)
    all_to_all x1, waiting for transfers between devices, exchange(): got = lax.all_to_all(send, 'var', split_axis=0, concat_axis=0, tiled=True)  74.1 us
    all_to_all x1, waiting for transfers between devices, local(): lax.all_to_all(received, 'tp', split_axis=0, concat_axis=0, tiled=True)  41.3 us
    pallas_call x1, Pallas kernels, mixer_of(): pl.pallas_call(functools.partial(mixer_kernel, dims), out_shape=jax.Shape...  16.5 us
    all_to_all x1, starting transfers between devices, local(): lax.all_to_all(received, 'tp', split_axis=0, concat_axis=0, tiled=True)  14.4 us
    all_to_all x1, starting transfers between devices, exchange(): got = lax.all_to_all(send, 'var', split_axis=0, concat_axis=0, tiled=True)  10.5 us
    all_gather x1, waiting for transfers between devices, local(): params = lax.all_gather(params, 'tp', axis=0)  4.11 us
  transfers between devices with their start and end apart: 3, of which 3 were waited for; matrix products, arithmetic and copies ran while one was open for 2% of the time, Pallas kernels for 0%

profile of v1, /device:TPU:1, one launch (start us, length us, event | category | flops | bytes accessed | tf_op | source)
XLA Modules:
  0.0 191.4 jit_solution(11398007946991947166)
XLA Ops:
  6.5 0.5 broadcast.65
  7.0 1.3 reduce.3
  8.4 0.1 reshape_squeeze.3
  8.5 0.2 reduce_window_sum.11
  8.7 0.8 broadcast_in_dim.17
  9.4 0.1 select_reduce_fusion
  9.5 0.1 copy.12
  9.6 0.1 reshape.91
  9.8 1.3 broadcast_in_dim.16.skip_ref
  11.1 2.8 %owner.1 = (bf16[6,72,128]{2,1,0:T(8,128)(2,1)}, bf16[6,128,128]{2,1,0:T(8,128)(2,1)}, bf16[72,512]{1,0:T(8,128)(2,1)}) custom-call(bf16[6,127,512]{2,1,0:T(8,128)(2,1)} %history_ref.1, bf16[6,6,3,512]{3,2,1,0:T(4,128)(2,1)} %inputs_ref.1, bf16[32,128]{1,0:T(8,128)(2,1)} %bitcast.31, bf16[3,7,512]{2,1,0:T(8,128)(2,1)} %bitcast.29, ...), custom_call_target="tpu_custom_call" | custom-call | tf_op jit(solution)/shard_map/owner/pallas_call | solution.py:77
  13.8 1.0 pad_maximum_fusion
  14.8 2.7 %gather_fusion = bf16[64,200,128]{2,1,0:T(8,128)(2,1)} fusion(bf16[6,200,128]{2,1,0:T(8,128)(2,1)S(1)} %pad_maximum_fusion, s32[1024]{0:T(1024)S(1)} %pad_clamp_fusion.1), kind=kCustom, calls=%fused_computation | custom fusion | bytes 6553856 | tf_op jit(solution)/shard_map/gather | solution.py:210
  17.5 10.5 %all-to-all-start = ((bf16[32,400,128]{2,1,0:T(8,128)(2,1)}), bf16[32,400,128]{2,1,0:T(8,128)(2,1)S(1)}, u32[]{:S(2)}, u32[]{:S(2)}) async-start(bf16[32,400,128]{2,1,0:T(8,128)(2,1)} %bitcast.22), calls=%async_computation | async-start | bytes 6553600 | tf_op jit(solution)/shard_map/all_to_all | solution.py:212
  28.0 0.2 convert_reduce_fusion
  28.2 74.1 %all-to-all-done = bf16[32,400,128]{2,1,0:T(8,128)(2,1)S(1)} async-done(((bf16[32,400,128]{2,1,0:T(8,128)(2,1)}), bf16[32,400,128]{2,1,0:T(8,128)(2,1)S(1)}, u32[]{:S(2)}, u32[]{:S(2)}) %all-to-all-start) | async-done | bytes 3276832 | tf_op jit(solution)/shard_map/all_to_all | solution.py:212
  102.4 0.0 copy-start
  102.4 0.0 copy-start.1
  102.4 2.0 %gather_fusion.1 = bf16[32,200,128]{2,1,0:T(8,128)(2,1)} fusion(bf16[64,200,128]{2,1,0:T(8,128)(2,1)S(1)} %bitcast.23, s32[1024]{0:T(1024)S(1)} %pad_clamp_fusion), kind=kCustom, calls=%fused_computation.1 | custom fusion | bytes 3276928 | tf_op jit(solution)/shard_map/gather | solution.py:218
  104.3 14.4 %all-to-all-start.1 = ((bf16[16,400,128]{2,1,0:T(8,128)(2,1)}), bf16[16,400,128]{2,1,0:T(8,128)(2,1)S(1)}, u32[]{:S(2)}, u32[]{:S(2)}) async-start(bf16[16,400,128]{2,1,0:T(8,128)(2,1)} %bitcast.26), calls=%async_computation.1 | async-start | bytes 3276800 | tf_op jit(solution)/shard_map/all_to_all | solution.py:252
  118.7 0.0 all-gather.3.cloned.1.call-start
  118.8 0.7 all-gather.3.cloned.1.call-update
  119.5 0.0 copy-done
  119.5 0.6 dynamic_slice.10.pos_ref
  120.1 0.0 copy-done.1
  120.1 0.6 dynamic_slice.11.allele_ref
  120.7 41.3 %all-to-all-done.1 = bf16[16,400,128]{2,1,0:T(8,128)(2,1)S(1)} async-done(((bf16[16,400,128]{2,1,0:T(8,128)(2,1)}), bf16[16,400,128]{2,1,0:T(8,128)(2,1)S(1)}, u32[]{:S(2)}, u32[]{:S(2)}) %all-to-all-start.1) | async-done | bytes 1638432 | tf_op jit(solution)/shard_map/all_to_all | solution.py:252
  162.0 1.1 slice.13.carried_ref
  163.1 0.9 slice.12.lead_ref
  164.0 4.1 %all-gather.3.cloned.1.call-done = bf16[1152,512]{1,0:T(8,128)(2,1)} async-done(((bf16[72,512]{1,0:T(8,128)(2,1)}), bf16[1152,512]{1,0:T(8,128)(2,1)}) %all-gather.3.cloned.1.call-update) | async-done | bytes 1179664 | tf_op jit(solution)/shard_map/all_gather | solution.py:254
  168.1 16.5 %mixer.1 = bf16[2,32,8192]{2,1,0:T(8,128)(2,1)} custom-call(s32[2]{0:T(128)} %dynamic_slice.10.pos_ref, s32[2]{0:T(128)} %dynamic_slice.11.allele_ref, bf16[2,3,32,8192]{3,2,1,0:T(8,128)(2,1)} %bitcast.27, bf16[16,2,72,128]{3,2,1,0:T(8,128)(2,1)} %slice.12.lead_ref, bf16[16,2,128,128]{3,2,1,0:T(8,128)(2,1)} %slice.13.carried_ref, bf16[16,72,512]{2,1,0:T(8,128)(2,1)} %bitcast.28), custom_call_target="tpu_custom_call" | custom-call | tf_op jit(solution)/shard_map/mixer/pallas_call | solution.py:194
  (7 shorter events, 0.1 us)
Async XLA Ops:
  17.5 84.9 %all-to-all-start = ((bf16[32,400,128]{2,1,0:T(8,128)(2,1)}), bf16[32,400,128]{2,1,0:T(8,128)(2,1)S(1)}, u32[]{:S(2)}, u32[]{:S(2)}) async-start(bf16[32,400,128]{2,1,0:T(8,128)(2,1)} %bitcast.22), calls=%async_computation | async-start | bytes 6553600 | tf_op jit(solution)/shard_map/all_to_all | solution.py:212
  102.4 17.1 %copy-start = (s32[32]{0:T(128)S(1)}, s32[32]{0:T(128)}, u32[]{:S(2)}) copy-start(s32[32]{0:T(128)} %param.20) | copy-start | bytes 388
  102.4 17.7 %copy-start.1 = (s32[32]{0:T(128)S(1)}, s32[32]{0:T(128)}, u32[]{:S(2)}) copy-start(s32[32]{0:T(128)} %param.21) | copy-start | bytes 388
  104.3 57.6 %all-to-all-start.1 = ((bf16[16,400,128]{2,1,0:T(8,128)(2,1)}), bf16[16,400,128]{2,1,0:T(8,128)(2,1)S(1)}, u32[]{:S(2)}, u32[]{:S(2)}) async-start(bf16[16,400,128]{2,1,0:T(8,128)(2,1)} %bitcast.26), calls=%async_computation.1 | async-start | bytes 3276800 | tf_op jit(solution)/shard_map/all_to_all | solution.py:252
  118.7 49.3 %all-gather.3.cloned.1.call-start = ((), (), s32[]{:S(2)}) async-start(), calls=%async_computation.2 | async-start | bytes 1253376 | tf_op jit(solution)/shard_map/all_gather | solution.py:254
Sparse Core Ops, SparseCore 0:
  121.7 46.3 all-gather.2
